TPU v7x, 512 devices: a whole 4x4x16 slice. The times are simulated.
512 devices in a mesh: gx: 16 (over y, z_lo), gy: 8 (over x, core), gz: 4 (over z_hi).
Axes of the slice: x: 4, y: 4, z: 16 (z_hi: 4, z_lo: 4; z = z_hi * 4 + z_lo), core: 2. Of those that a mesh axis runs over, the one named last changes fastest.
Arguments:
- positions: float32 [16, 8, 4, 3, 64], P('gx', 'gy', 'gz'), may hold values from 0 to 5
- species: int32 [16, 8, 4, 64], P('gx', 'gy', 'gz'), may hold values from 0 to 7
- counts: int32 [16, 8, 4], P('gx', 'gy', 'gz'), may hold values from 4 to 64, as said below
- embed: bfloat16 [8, 128], replicated, may hold values from -6 to 6
- radial_one: float32 [2, 4, 128], replicated, may hold values from -6 to 6
- mix_one: bfloat16 [128, 256], replicated, may hold values from -0.375 to 0.375
- read_one: float32 [128], replicated, may hold values from -0.5 to 0.5
- radial_two: float32 [4, 128], replicated, may hold values from -6 to 6
- mix_two: bfloat16 [128, 128], replicated, may hold values from -0.5 to 0.5
- read_hidden: bfloat16 [16, 128], replicated, may hold values from -0.5 to 0.5
- read_out: float32 [16], replicated, may hold values from -1.5 to 1.5
Outputs:
- forces: float32 [16, 8, 4, 3, 64], P('gx', 'gy', 'gz')
- energies: float32 [16, 8, 4, 64], P('gx', 'gy', 'gz')
- features: bfloat16 [16, 8, 4, 128, 64], P('gx', 'gy', 'gz')
Inputs may be any that keep to these rules, and one draw needn't show every extreme that they name: `counts`: the first block of the grid holds exactly 64 live atoms.
All inputs are finite; a program needn't handle non-finite values.
Results may differ from a plain program's by a relative error of at most 0.018.
Values may be sent and summed in bfloat16 or wider, within the bound.
A program may use at most 64 MiB of HBM per device.

v0:
```python
import functools
import math

import jax
import jax.numpy as jnp
from jax import lax
from jax.experimental import pallas as pl
from jax.experimental.pallas import tpu as pltpu
from jax.sharding import PartitionSpec as P

CELL_SIDE = 5.0
CUT_SQUARE = 25.0
SOFTEN = 0.25
MSG_SCALE = 0.05
ROOT_THREE = math.sqrt(3.0)
WAVE = math.pi / CELL_SIDE
FAR = 1000.0
MESH = pl.DeviceIdType.MESH
OFFSETS = 27
CENTRE = 13
CHUNKS = 14
LANES = 128
PIECE = 16
COMPACT = True
BF16 = jnp.bfloat16
F32 = jnp.float32


def nt(a, b):
    return lax.dot_general(a, b, (((1,), (1,)), ((), ())), preferred_element_type=F32)


def nn(a, b):
    return jnp.dot(a, b, preferred_element_type=F32)


def sigmoid(v):
    return 1.0 / (1.0 + jnp.exp(-v))


def silu_slope(v, s):
    return s * (1.0 + v * (1.0 - s))


def cos_sin(y):
    q = y * y
    c = 1.0 / 479001600.0
    for term in (-1.0 / 3628800.0, 1.0 / 40320.0, -1.0 / 720.0, 1.0 / 24.0, -0.5, 1.0):
        c = c * q + term
    s = -1.0 / 39916800.0
    for term in (1.0 / 362880.0, -1.0 / 5040.0, 1.0 / 120.0, -1.0 / 6.0, 1.0):
        s = s * q + term
    return c, s * y


def block_of(gx, gy, gz, shape):
    nx, _, nz = shape
    if not COMPACT:
        return gx, gy, gz
    run = nx // nz
    return gz * run + lax.rem(gx, run), gy, gx // run


def kernel(
    shape,
    packet,
    embed,
    radial_one,
    mix_one,
    read_one,
    radial_two,
    mix_two,
    read_hidden,
    read_out_col,
    read_out_row,
    out,
    feats,
    slots,
    halo,
    mine,
    ghosts_out,
    ghosts_in,
    own,
    diag,
    vs,
    sm,
    hot,
    pre,
    d1,
    acc,
    pair_lhs,
    send,
    recv,
):
    nx, ny, nz = shape
    here = block_of(lax.axis_index("gx"), lax.axis_index("gy"), lax.axis_index("gz"), shape)

    def offset_of(t):
        return t + jnp.where(t >= CENTRE, 1, 0)

    def parts(o):
        return o // 9 - 1, lax.rem(o // 3, 3) - 1, lax.rem(o, 3) - 1

    def device(o, sign):
        ox, oy, oz = parts(o)
        bx = lax.rem(here[0] + sign * ox + nx, nx)
        by = lax.rem(here[1] + sign * oy + ny, ny)
        bz = lax.rem(here[2] + sign * oz + nz, nz)
        return block_of(bx, by, bz, shape)

    def copy_of(phase, o, sign):
        if phase == 0:
            src, dst = packet, slots.at[o]
        elif phase == 3:
            src, dst = ghosts_out.at[o // 2], ghosts_in.at[o]
        else:
            half = pl.ds((phase - 1) * LANES, LANES)
            src, dst = mine.at[phase - 1], halo.at[pl.ds(o * 64, 64), half]
        return pltpu.make_async_remote_copy(
            src_ref=src,
            dst_ref=dst,
            send_sem=send.at[phase, o],
            recv_sem=recv.at[phase, o],
            device_id=device(o, sign),
            device_id_type=MESH,
        )

    def start_all(phase, sign):
        def step(t, carry):
            copy_of(phase, offset_of(t), sign).start()
            return carry

        lax.fori_loop(0, OFFSETS - 1, step, 0)

    def arrived_all(phase, sign):
        def step(t, carry):
            copy_of(phase, offset_of(t), sign).wait_recv()
            return carry

        lax.fori_loop(0, OFFSETS - 1, step, 0)

    def sent_all(phase, sign):
        def step(t, carry):
            copy_of(phase, offset_of(t), sign).wait_send()
            return carry

        lax.fori_loop(0, OFFSETS - 1, step, 0)

    barrier = pltpu.get_barrier_semaphore()

    def greet(t, carry):
        pl.semaphore_signal(
            barrier, inc=1, device_id=device(offset_of(t), 1), device_id_type=MESH
        )
        return carry

    lax.fori_loop(0, OFFSETS - 1, greet, 0)

    mine_packet = packet[...]
    column = jnp.transpose(mine_packet)[0:64, :]
    live_col = jnp.where(column[:, 3:4] >= 0.0, 1.0, 0.0)
    for k in range(3):
        place = jnp.where(live_col > 0.0, column[:, k : k + 1], -FAR)
        own[k] = jnp.broadcast_to(place, (64, LANES))
    live_row = jnp.where(mine_packet[3:4, 0:64] >= 0.0, 1.0, 0.0)
    row_id = lax.broadcasted_iota(jnp.int32, (64, LANES), 0)
    lane_id = lax.broadcasted_iota(jnp.int32, (64, LANES), 1)
    diag[...] = jnp.where(row_id + 64 == lane_id, CUT_SQUARE, 0.0)
    species_id = lax.broadcasted_iota(jnp.int32, (64, 8), 1).astype(F32)
    own_hot = jnp.where(column[:, 3:4] == species_id, 1.0, 0.0).astype(BF16)
    embed_wide = embed[...].astype(F32)
    own_embed = nn(own_hot, embed[...])
    tables = []
    for g in range(2):
        rows = [radial_one[g, n : n + 1, :] * embed_wide for n in range(4)]
        tables.append(jnp.concatenate(rows, axis=0).astype(BF16))
    table_scalar, table_vector = tables
    slots[CENTRE] = mine_packet
    pad_row = lax.broadcasted_iota(jnp.int32, (8, LANES), 0)
    slots[OFFSETS] = jnp.where(pad_row < 3, FAR, -1.0)
    halo[OFFSETS * 64 :, :] = jnp.zeros((64, 2 * LANES), BF16)
    low = lax.broadcasted_iota(jnp.int32, (1, LANES), 1) < 64
    hot_row = lax.broadcasted_iota(jnp.int32, (32, LANES), 0).astype(F32)

    pl.semaphore_wait(barrier, OFFSETS - 1)
    start_all(0, -1)
    arrived_all(0, -1)

    def far_rows(m):
        first, second = slots[2 * m], slots[2 * m + 1]
        shift_first, shift_second = parts(2 * m), parts(2 * m + 1)
        rows = []
        for k in range(3):
            a = first[k : k + 1, :] + shift_first[k].astype(F32) * CELL_SIDE
            b = second[k : k + 1, :] + shift_second[k].astype(F32) * CELL_SIDE
            rows.append(jnp.where(low, a, b))
        return rows, jnp.where(low, first[3:4, :], second[3:4, :])

    def geometry(places, m, top):
        rows = pl.ds(top, PIECE)
        sep = [places[k] - own[k, rows, :] for k in range(3)]
        dist = sep[0] * sep[0] + sep[1] * sep[1] + sep[2] * sep[2] + SOFTEN
        self_pair = jnp.where(m == CENTRE // 2, 1.0, 0.0)
        dist = jnp.minimum(dist + diag[rows, :] * self_pair, CUT_SQUARE)
        inverse = lax.rsqrt(dist)
        edge = (CUT_SQUARE - dist) * (1.0 / CUT_SQUARE)
        angle = dist * inverse * WAVE - 0.5 * math.pi
        sine, minus_cosine = cos_sin(angle)
        double = -2.0 * minus_cosine
        sines = [sine, double * sine]
        sines.append(double * sines[1] - sines[0])
        sines.append(double * sines[2] - sines[1])
        return sep, inverse, edge, sines, double

    def forward(m, carry):
        places, kinds = far_rows(m)
        for n in range(4):
            hit = jnp.where(kinds == hot_row - 8.0 * n, 1.0, 0.0).astype(BF16)
            hot[:, pl.ds(pl.multiple_of(m * 512 + n * LANES, LANES), LANES)] = hit
        for top in range(0, 64, PIECE):
            sep, inverse, edge, sines, _ = geometry(places, m, top)
            weight = edge * edge * inverse
            scaled = inverse * ROOT_THREE
            units = [s * scaled for s in sep]
            for n in range(4):
                basis = sines[n] * weight
                narrow = basis.astype(BF16)
                wide_cols = pl.ds(pl.multiple_of(m * 512 + n * LANES, LANES), LANES)
                cols = pl.ds(pl.multiple_of(m * LANES, LANES), LANES)
                sm[n * 64 + top : n * 64 + top + PIECE, cols] = narrow
                vs[top : top + PIECE, wide_cols] = narrow
                for k in range(3):
                    at = 64 * (k + 1) + top
                    vs[at : at + PIECE, wide_cols] = (units[k] * basis).astype(BF16)
        return carry

    lax.fori_loop(0, CHUNKS, forward, 0)

    def gather_kinds(j, total):
        cols = pl.ds(pl.multiple_of(j * 1024, 1024), 1024)
        return total + nt(vs[:, cols], hot[:, cols])

    kinds_sum = lax.fori_loop(0, 7, gather_kinds, jnp.zeros((256, 32), F32))
    high = kinds_sum.astype(BF16)
    rest = (kinds_sum - high.astype(F32)).astype(BF16)
    scalar_msg = MSG_SCALE * (nn(high[0:64], table_scalar) + nn(rest[0:64], table_scalar))
    vector_msg = MSG_SCALE * (nn(high[64:], table_vector) + nn(rest[64:], table_vector))
    squares = vector_msg * vector_msg
    norm = squares[0:64] + squares[64:128] + squares[128:192]
    invariants = jnp.concatenate([scalar_msg, norm], axis=1).astype(BF16)
    mixing = nt(invariants, mix_one[...])
    gate = sigmoid(mixing)
    layer_one = (own_embed + mixing * gate).astype(BF16)
    mine[0] = layer_one
    halo[CENTRE * 64 : CENTRE * 64 + 64, 0:LANES] = layer_one
    start_all(1, -1)

    def slopes(m, carry):
        places, _ = far_rows(m)
        cols = pl.ds(pl.multiple_of(m * LANES, LANES), LANES)
        for top in range(0, 64, PIECE):
            sep, inverse, edge, sines, double = geometry(places, m, top)
            weight = edge * edge * inverse
            fall = -edge * (4.0 / CUT_SQUARE + edge * inverse * inverse)
            cosines = [0.5 * double, 0.5 * double * double - 1.0]
            cosines.append(double * cosines[1] - cosines[0])
            cosines.append(double * cosines[2] - cosines[1])
            rows = pl.ds(top, PIECE)
            for k in range(3):
                pre[k, rows, cols] = sep[k]
            pre[3, rows, cols] = inverse
            for n in range(4):
                pre[4 + n, rows, cols] = sines[n] * weight
                turn = cosines[n] * ((n + 1) * WAVE)
                pre[8 + n, rows, cols] = turn * weight + sines[n] * fall
        return carry

    lax.fori_loop(0, CHUNKS, slopes, 0)
    arrived_all(1, -1)

    def spread(half):
        def step(j, total):
            rows = pl.ds(pl.multiple_of(j * 256, 256), 256)
            return total + nn(sm[:, rows], halo[rows, half * LANES : (half + 1) * LANES])

        total = lax.fori_loop(0, 7, step, jnp.zeros((256, LANES), F32))
        result = None
        for n in range(4):
            term = total[n * 64 : n * 64 + 64] * (MSG_SCALE * radial_two[n : n + 1, :])
            result = term if result is None else result + term
        return result

    rounded_two = spread(0).astype(BF16)
    mixing_two = nt(rounded_two, mix_two[...])
    gate_two = sigmoid(mixing_two)
    layer_wide = layer_one.astype(F32)
    features = (layer_wide + mixing_two * gate_two).astype(BF16)
    hidden = nt(features, read_hidden[...])
    slope = silu_slope(hidden, sigmoid(hidden)) * read_out_row[...] * live_col
    feature_adjoint = nn(slope.astype(BF16), read_hidden[...])
    mixing_adjoint = (feature_adjoint * silu_slope(mixing_two, gate_two)).astype(BF16)
    rounded_adjoint = nn(mixing_adjoint, mix_two[...]).astype(BF16)
    mine[1] = rounded_adjoint
    halo[CENTRE * 64 : CENTRE * 64 + 64, LANES:] = rounded_adjoint
    start_all(2, -1)

    feats[...] = jnp.transpose(features.astype(F32)).astype(BF16)
    hidden_row = nt(read_hidden[...], features)
    second = jnp.sum(hidden_row * sigmoid(hidden_row) * read_out_col[...], axis=0, keepdims=True)
    first = jnp.sum(jnp.transpose(layer_wide * read_one[...]), axis=0, keepdims=True)
    energy = (first + second) * live_row
    adjoint_wide = rounded_adjoint.astype(F32)
    for n in range(4):
        scale = MSG_SCALE * radial_two[n : n + 1, :]
        pair_lhs[n * 64 : n * 64 + 64, 0:LANES] = (scale * adjoint_wide).astype(BF16)
        pair_lhs[n * 64 : n * 64 + 64, LANES:] = (scale * layer_wide).astype(BF16)
    acc[...] = jnp.zeros((3, 64, LANES), F32)
    arrived_all(2, -1)

    layer_adjoint = feature_adjoint + read_one[...] * live_col + spread(1)
    mixing_one_adjoint = (layer_adjoint * silu_slope(mixing, gate)).astype(BF16)
    invariant_adjoint = nn(mixing_one_adjoint, mix_one[...])
    scalar_adjoint = (MSG_SCALE * invariant_adjoint[:, 0:LANES]).astype(BF16)
    norm_adjoint = (2.0 * MSG_SCALE) * invariant_adjoint[:, LANES:]
    vector_adjoint = jnp.concatenate(
        [vector_msg[k * 64 : k * 64 + 64] * norm_adjoint for k in range(3)], axis=0
    ).astype(BF16)
    kinds_adjoint = jnp.concatenate(
        [nt(scalar_adjoint, table_scalar), nt(vector_adjoint, table_vector)], axis=0
    ).astype(BF16)

    def backward_one(m, carry):
        wide_cols = pl.ds(pl.multiple_of(m * 512, 512), 512)
        cols = pl.ds(pl.multiple_of(m * LANES, LANES), LANES)
        d1[...] = nn(kinds_adjoint, hot[:, wide_cols])
        ghost = [jnp.zeros((PIECE, LANES), F32) for _ in range(3)]
        for top in range(0, 64, PIECE):
            rows = pl.ds(top, PIECE)
            sep = [pre[k, rows, cols] for k in range(3)]
            inverse = pre[3, rows, cols]
            scaled = inverse * ROOT_THREE
            along, across = None, None
            turned = [None, None, None]
            for n in range(4):
                basis, slope_n = pre[4 + n, rows, cols], pre[8 + n, rows, cols]
                lanes = slice(n * LANES, (n + 1) * LANES)
                pulls = [
                    d1[64 * (k + 1) + top : 64 * (k + 1) + top + PIECE, lanes] for k in range(3)
                ]
                projected = sep[0] * pulls[0] + sep[1] * pulls[1] + sep[2] * pulls[2]
                push = (d1[top : top + PIECE, lanes] + scaled * projected) * slope_n
                along = push if along is None else along + push
                lean = basis * projected
                across = lean if across is None else across + lean
                for k in range(3):
                    term = basis * pulls[k]
                    turned[k] = term if turned[k] is None else turned[k] + term
            radial = inverse * (along - scaled * inverse * across)
            for k in range(3):
                grad = sep[k] * radial + scaled * turned[k]
                ghost[k] = ghost[k] + grad
                acc[k, rows, :] = acc[k, rows, :] - grad
        for k in range(3):
            ghosts_out[m, k : k + 1, :] = jnp.sum(ghost[k], axis=0, keepdims=True)
        return carry

    ghosts_out[...] = jnp.zeros((CHUNKS, 8, LANES), F32)
    lax.fori_loop(0, CHUNKS, backward_one, 0)
    ghosts_in[CENTRE] = ghosts_out[CENTRE // 2]
    start_all(3, 1)

    def backward_two(m, carry):
        cols = pl.ds(pl.multiple_of(m * LANES, LANES), LANES)
        d1[:, 0:LANES] = nt(pair_lhs[...], halo[cols, :])
        for top in range(0, 64, PIECE):
            rows = pl.ds(top, PIECE)
            along = None
            for n in range(4):
                push = d1[n * 64 + top : n * 64 + top + PIECE, 0:LANES] * pre[8 + n, rows, cols]
                along = push if along is None else along + push
            along = along * pre[3, rows, cols]
            for k in range(3):
                acc[k, rows, :] = acc[k, rows, :] - along * pre[k, rows, cols]
        return carry

    lax.fori_loop(0, CHUNKS, backward_two, 0)
    sums = [jnp.sum(jnp.transpose(acc[k]), axis=0, keepdims=True) for k in range(3)]
    arrived_all(3, 1)

    even, odd = ghosts_in[0], ghosts_in[1]
    for o in range(2, OFFSETS):
        if o % 2:
            odd = odd + ghosts_in[o]
        else:
            even = even + ghosts_in[o]
    for k in range(3):
        back = even[k : k + 1, 0:64] + odd[k : k + 1, 64:LANES]
        out[k : k + 1, :] = -(sums[k] + back)
    out[3:4, :] = energy

    for phase, sign in ((0, -1), (1, -1), (2, -1), (3, 1)):
        sent_all(phase, sign)


def permutation(shape):
    nx, _, nz = shape
    run = nx // nz
    pairs = []
    for gx in range(nx):
        for gz in range(nz):
            to_x, to_z = gz * run + gx % run, gx // run
            pairs.append((gx * nz + gz, to_x * nz + to_z))
    return pairs


def local(
    shape,
    positions,
    species,
    counts,
    embed,
    radial_one,
    mix_one,
    read_one,
    radial_two,
    mix_two,
    read_hidden,
    read_out,
):
    slots = positions.shape[-1]
    occupied = (jnp.arange(slots) < counts[0, 0, 0])[None, :]
    places = jnp.where(occupied, positions[0, 0, 0], FAR)
    kinds = jnp.where(occupied, species[0, 0], -1).astype(F32)
    packet = jnp.concatenate([places, kinds, jnp.zeros((4, slots), F32)], axis=0)
    packet = jnp.concatenate([packet, packet], axis=1)

    def moved(value):
        return lax.ppermute(value, ("gx", "gz"), permutation(shape)) if COMPACT else value

    packet = moved(packet)
    vmem = pl.BlockSpec(memory_space=pltpu.VMEM)
    out, feats = pl.pallas_call(
        functools.partial(kernel, shape),
        out_shape=(
            jax.ShapeDtypeStruct((4, slots), F32),
            jax.ShapeDtypeStruct((LANES, slots), BF16),
        ),
        in_specs=[vmem] * 10,
        out_specs=(vmem, vmem),
        scratch_shapes=[
            pltpu.VMEM((OFFSETS + 1, 8, LANES), F32),
            pltpu.VMEM((CHUNKS * LANES, 2 * LANES), BF16),
            pltpu.VMEM((2, 64, LANES), BF16),
            pltpu.VMEM((CHUNKS, 8, LANES), F32),
            pltpu.VMEM((OFFSETS, 8, LANES), F32),
            pltpu.VMEM((3, 64, LANES), F32),
            pltpu.VMEM((64, LANES), F32),
            pltpu.VMEM((256, CHUNKS * 512), BF16),
            pltpu.VMEM((256, CHUNKS * LANES), BF16),
            pltpu.VMEM((32, CHUNKS * 512), BF16),
            pltpu.VMEM((12, 64, CHUNKS * LANES), F32),
            pltpu.VMEM((256, 512), F32),
            pltpu.VMEM((3, 64, LANES), F32),
            pltpu.VMEM((256, 2 * LANES), BF16),
            pltpu.SemaphoreType.DMA((4, OFFSETS)),
            pltpu.SemaphoreType.DMA((4, OFFSETS)),
        ],
        compiler_params=pltpu.CompilerParams(
            collective_id=0, has_side_effects=True, vmem_limit_bytes=40 * 1024 * 1024
        ),
        name="potential",
    )(
        packet,
        embed,
        radial_one,
        mix_one,
        read_one[None, :],
        radial_two,
        mix_two,
        read_hidden,
        read_out[:, None],
        read_out[None, :],
    )
    out, feats = moved(out), moved(feats)
    return (out[None, None, None, 0:3], out[None, None, None, 3], feats[None, None, None])


def solution(mesh):
    shape = tuple(mesh.shape[name] for name in ("gx", "gy", "gz"))
    block = ("gx", "gy", "gz")
    in_specs = (P(*block, None, None), P(*block, None), P(*block)) + (P(),) * 8
    out_specs = (P(*block, None, None), P(*block, None), P(*block, None, None))
    step = functools.partial(local, shape)
    return jax.shard_map(step, mesh=mesh, in_specs=in_specs, out_specs=out_specs, check_vma=False)
```

profile of v0, /device:TPU:16, one launch (start us, length us, event | category | flops | bytes accessed | tf_op | source)
XLA Modules:
  0.0 101.1 jit_solution(2048317485389694560)
XLA Ops:
  0.6 0.0 copy-start.1
  1.3 0.7 fusion
  2.0 0.7 bitcast_select_fusion
  2.7 0.1 maximum_maximum_fusion
  2.7 15.5 %collective-permute-start = (f32[8,128]{1,0:T(8,128)S(1)}, f32[8,128]{1,0:T(8,128)S(1)}, u32[]{:S(2)}, u32[]{:S(2)}) collective-permute-start(f32[8,128]{1,0:T(8,128)S(1)} %maximum_maximum_fusion), channel_id=1, source_target_pairs={{0,0},{1,128},{2,256},{3,384},{32,32},{33,160},{34,288},{35,416},{... | collective-permute-start | bytes 12296 | tf_op jit(solution)/shard_map/ppermute | solution.py:438
  18.2 0.0 copy-start.2
  18.2 0.7 copy.14.read_out_col
  19.0 0.0 copy-start.4
  19.0 0.8 collective-permute-done.packet
  19.8 0.0 copy-start.6
  19.8 0.0 copy-done.1
  19.8 0.0 copy-done.2
  19.8 0.0 copy-done.4
  19.8 0.6 copy-done.6
  20.5 0.0 copy-start
  20.5 0.8 copy-done
  21.3 0.0 copy-start.3
  21.3 0.7 copy-done.3
  22.0 0.0 copy-start.5
  22.0 0.7 copy-done.5
  22.7 0.0 copy-start.7
  22.7 0.7 copy-done.7
  23.3 50.7 %potential.1 = (f32[4,64]{1,0:T(4,128)S(1)}, bf16[128,64]{1,0:T(8,128)(2,1)S(1)}) custom-call(f32[8,128]{1,0:T(8,128)S(1)} %collective-permute-done.packet, bf16[8,128]{1,0:T(8,128)(2,1)S(1)} %copy-done.4, f32[2,4,128]{2,1,0:T(4,128)S(1)} %copy-done.2, bf16[128,256]{1,0:T(8,128)(2,1)S(1)} %copy-done, f32[1,128]{1,0:T(1,128)S(1)} %bitcast.17, ...), custom_call_target="tpu_custom_call" | custom-call | tf_op jit(solution)/shard_map/potential/pallas_call | solution.py:442
  74.0 9.5 %collective-permute-start.1 = (f32[4,64]{1,0:T(4,128)S(1)}, f32[4,64]{1,0:T(4,128)S(1)}, u32[]{:S(2)}, u32[]{:S(2)}) collective-permute-start(f32[4,64]{1,0:T(4,128)S(1)} %get-tuple-element.5), channel_id=1, source_target_pairs={{0,0},{1,128},{2,256},{3,384},{32,32},{33,160},{34,288},{35,416},{... | collective-permute-start | bytes 3080 | tf_op jit(solution)/shard_map/ppermute | solution.py:438
  83.5 7.5 %collective-permute-start.2 = (bf16[128,64]{1,0:T(8,128)(2,1)S(1)}, bf16[128,64]{1,0:T(8,128)(2,1)S(1)}, u32[]{:S(2)}, u32[]{:S(2)}) collective-permute-start(bf16[128,64]{1,0:T(8,128)(2,1)S(1)} %get-tuple-element.6), channel_id=1, source_target_pairs={{0,0},{1,128},{2,256},{3,384},{32,32},{33,160},{34,288},{35,416},{... | collective-permute-start | bytes 49160 | tf_op jit(solution)/shard_map/ppermute | solution.py:438
  91.0 0.0 collective-permute-done.1
  91.0 0.5 slice_bitcast_fusion.1
  91.5 0.6 copy.15
  92.1 8.4 %collective-permute-done.2 = bf16[128,64]{1,0:T(8,128)(2,1)S(1)} collective-permute-done((bf16[128,64]{1,0:T(8,128)(2,1)S(1)}, bf16[128,64]{1,0:T(8,128)(2,1)S(1)}, u32[]{:S(2)}, u32[]{:S(2)}) %collective-permute-start.2) | collective-permute-done | bytes 16416 | tf_op jit(solution)/shard_map/ppermute | solution.py:438
  100.5 0.7 copy.16
  (3 shorter events, 0.0 us)
Async XLA Ops:
  0.6 19.2 %copy-start.1 = (bf16[128,128]{1,0:T(8,128)(2,1)S(1)}, bf16[128,128]{1,0:T(8,128)(2,1)}, u32[]{:S(2)}) copy-start(bf16[128,128]{1,0:T(8,128)(2,1)} %mix_two.1) | copy-start | bytes 98308
  2.7 17.1 %collective-permute-start = (f32[8,128]{1,0:T(8,128)S(1)}, f32[8,128]{1,0:T(8,128)S(1)}, u32[]{:S(2)}, u32[]{:S(2)}) collective-permute-start(f32[8,128]{1,0:T(8,128)S(1)} %maximum_maximum_fusion), channel_id=1, source_target_pairs={{0,0},{1,128},{2,256},{3,384},{32,32},{33,160},{34,288},{35,416},{... | collective-permute-start | bytes 12296 | tf_op jit(solution)/shard_map/ppermute | solution.py:438
  18.2 1.6 %copy-start.2 = (f32[2,4,128]{2,1,0:T(4,128)S(1)}, f32[2,4,128]{2,1,0:T(4,128)}, u32[]{:S(2)}) copy-start(f32[2,4,128]{2,1,0:T(4,128)} %radial_one.1) | copy-start | bytes 12292
  19.0 0.8 copy-start.4
  19.8 0.7 copy-start.6
  20.5 0.8 copy-start
  21.3 0.7 copy-start.3
  22.0 0.7 copy-start.5
  22.7 0.7 copy-start.7
  74.0 17.0 %collective-permute-start.1 = (f32[4,64]{1,0:T(4,128)S(1)}, f32[4,64]{1,0:T(4,128)S(1)}, u32[]{:S(2)}, u32[]{:S(2)}) collective-permute-start(f32[4,64]{1,0:T(4,128)S(1)} %get-tuple-element.5), channel_id=1, source_target_pairs={{0,0},{1,128},{2,256},{3,384},{32,32},{33,160},{34,288},{35,416},{... | collective-permute-start | bytes 3080 | tf_op jit(solution)/shard_map/ppermute | solution.py:438
  83.5 16.9 %collective-permute-start.2 = (bf16[128,64]{1,0:T(8,128)(2,1)S(1)}, bf16[128,64]{1,0:T(8,128)(2,1)S(1)}, u32[]{:S(2)}, u32[]{:S(2)}) collective-permute-start(bf16[128,64]{1,0:T(8,128)(2,1)S(1)} %get-tuple-element.6), channel_id=1, source_target_pairs={{0,0},{1,128},{2,256},{3,384},{32,32},{33,160},{34,288},{35,416},{... | collective-permute-start | bytes 49160 | tf_op jit(solution)/shard_map/ppermute | solution.py:438
where the time goes:
time: 102 us; the launch traced here: 101 us
  Pallas kernels  50.7 us (50%)
  starting transfers between devices  32.4 us (32%)
  waiting for transfers between devices  9.18 us (9%)
  local copies, waits for them, and re-layouts  6.03 us (6%)
  other arithmetic  1.43 us (1%)
  between operations  1.37 us (1%)
    pallas_call x1, Pallas kernels, local(): pl.pallas_call(functools.partial(kernel, shape), out_shape=(jax.ShapeDtyp...  50.7 us
    ppermute x3, starting transfers between devices, moved(): lax.ppermute(value, ('gx', 'gz'), permutation(shape))  32.4 us
    ppermute x3, waiting for transfers between devices, moved(): lax.ppermute(value, ('gx', 'gz'), permutation(shape))  9.18 us
    unnamed x18, local copies, waits for them, and re-layouts  4.78 us
  transfers between devices with their start and end apart: 3, of which 2 were waited for; matrix products, arithmetic and copies ran while one was open for 2% of the time, Pallas kernels for 0%

commit v1 on v0

v1 whole, which is shorter than its diff:
```python
import functools
import math

import jax
import jax.numpy as jnp
from jax import lax
from jax.experimental import pallas as pl
from jax.experimental.pallas import tpu as pltpu
from jax.sharding import PartitionSpec as P

CELL_SIDE = 5.0
CUT_SQUARE = 25.0
SOFTEN = 0.25
MSG_SCALE = 0.05
ROOT_THREE = math.sqrt(3.0)
WAVE = math.pi / CELL_SIDE
FAR = 1000.0
MESH = pl.DeviceIdType.MESH
OFFSETS = 27
CENTRE = 13
CHUNKS = 14
LANES = 128
PIECE = 16
COMPACT = True
BF16 = jnp.bfloat16
F32 = jnp.float32


def nt(a, b):
    return lax.dot_general(a, b, (((1,), (1,)), ((), ())), preferred_element_type=F32)


def nn(a, b):
    return jnp.dot(a, b, preferred_element_type=F32)


def sigmoid(v):
    return 1.0 / (1.0 + jnp.exp(-v))


def silu_slope(v, s):
    return s * (1.0 + v * (1.0 - s))


def cos_sin(y):
    q = y * y
    c = 1.0 / 479001600.0
    for term in (-1.0 / 3628800.0, 1.0 / 40320.0, -1.0 / 720.0, 1.0 / 24.0, -0.5, 1.0):
        c = c * q + term
    s = -1.0 / 39916800.0
    for term in (1.0 / 362880.0, -1.0 / 5040.0, 1.0 / 120.0, -1.0 / 6.0, 1.0):
        s = s * q + term
    return c, s * y


def corner(o):
    return o // 9 - 1, o // 3 % 3 - 1, o % 3 - 1


def kernel(
    shape,
    positions,
    species,
    counts,
    *refs,
):
    sources, refs = refs[:8], refs[8:]
    forces, energies, features_out = refs[:3]
    (
        embed,
        radial_one,
        mix_one,
        read_one,
        radial_two,
        mix_two,
        read_hidden,
        read_out,
    ) = refs[3:11]
    (
        packet,
        slots,
        halo,
        mine,
        sheet_out,
        sheet_in,
        ghosts_out,
        centre_out,
        ghosts_in,
        own,
        diag,
        vs,
        sm,
        hot,
        pre,
        d1,
        acc,
        pair_lhs,
        tally,
        send,
        recv,
        load,
    ) = refs[11:]
    nx, ny, nz = shape
    here = (lax.axis_index("gx"), lax.axis_index("gy"), lax.axis_index("gz"))

    run = nx // nz

    def near(index, size):
        return (
            jnp.where(index == 0, size - 1, index - 1),
            index,
            jnp.where(index == size - 1, 0, index + 1),
        )

    if COMPACT:
        block = (here[2] * run + lax.rem(here[0], run), here[1], here[0] // run)
    else:
        block = here
    block_near = [near(index, size) for index, size in zip(block, shape)]
    here_near = [near(index, size) for index, size in zip(here, shape)]

    def splits(three):
        return [(lax.rem(v, run), v // run) for v in three]

    def worker(triples, halves, o):
        ox, oy, oz = corner(o)
        bx, by, bz = triples[0][1 + ox], triples[1][1 + oy], triples[2][1 + oz]
        if not COMPACT:
            return bx, by, bz
        low_x, high_x = halves[1 + ox]
        return bz * run + low_x, by, high_x

    block_halves = splits(block_near[0]) if COMPACT else None
    here_halves = splits(here_near[0]) if COMPACT else None

    def holder(o):
        ox, oy, oz = corner(o)
        return block_near[0][1 + ox], block_near[1][1 + oy], block_near[2][1 + oz]

    def opposite(o):
        return OFFSETS - 1 - o

    def is_here(device):
        same = (device[0] == here[0]) & (device[1] == here[1])
        return same & (device[2] == here[2])

    to_worker = [worker(block_near, block_halves, opposite(o)) for o in range(OFFSETS)]
    packet_to = [worker(here_near, here_halves, opposite(o)) for o in range(OFFSETS)]
    holders = [holder(o) for o in range(OFFSETS)]
    neighbours = [o for o in range(OFFSETS) if o != CENTRE]
    farthest = sorted(neighbours, key=lambda o: -sum(abs(step) for step in corner(o)))
    selves = {}
    if COMPACT:
        for o in range(OFFSETS):
            if corner(o)[1] == 0 or ny < 3:
                selves[o] = is_here(holders[o])

    def elsewhere(o, action):
        if not COMPACT and o == CENTRE:
            return
        if o in selves:
            pl.when(jnp.logical_not(selves[o]))(action)
        else:
            action()

    def at_home(o, action):
        if not COMPACT and o == CENTRE:
            action()
        if o in selves:
            pl.when(selves[o])(action)

    def remote(src, dst, phase, o, device):
        return pltpu.make_async_remote_copy(
            src_ref=src,
            dst_ref=dst,
            send_sem=send.at[phase, o],
            recv_sem=recv.at[phase, o],
            device_id=device,
            device_id_type=MESH,
        )

    def coordinates(o):
        return remote(packet, slots.at[o], 0, o, packet_to[o])

    def channels(phase, o):
        dst = halo.at[phase - 1, pl.ds(o * 64, 64)]
        return remote(mine.at[phase - 1], dst, phase, o, to_worker[o])

    def ghosts(o):
        src = centre_out if o == CENTRE else ghosts_out.at[o]
        return remote(src, ghosts_in.at[o], 3, o, holders[o])

    def sheet():
        return remote(sheet_out, sheet_in, 1, CENTRE, holders[CENTRE])

    barrier = pltpu.get_barrier_semaphore()

    def greet(device):
        pl.semaphore_signal(barrier, inc=1, device_id=device, device_id_type=MESH)

    for o in range(OFFSETS):
        if COMPACT:
            elsewhere(o, functools.partial(greet, holders[o]))
    for o in neighbours:
        greet(to_worker[o])

    loads = []
    for i in range(8):
        dst = refs[3 + i]
        copy = pltpu.make_async_copy(sources[i], dst, load.at[i])
        copy.start()
        loads.append(copy)
    occupied = lax.broadcasted_iota(jnp.int32, (1, 64), 1) < counts[0, 0, 0]
    kinds = jnp.where(occupied, species[0, 0], -1).astype(F32)
    places = [jnp.where(occupied, positions[0, 0, k], FAR) for k in range(3)]
    packet[0:1, 0:64] = places[0]
    packet[0:1, 64:LANES] = places[1]
    packet[1:2, 0:64] = places[2]
    packet[1:2, 64:LANES] = kinds
    row_id = lax.broadcasted_iota(jnp.int32, (64, LANES), 0)
    lane_id = lax.broadcasted_iota(jnp.int32, (64, LANES), 1)
    diag[...] = jnp.where(row_id + 64 == lane_id, CUT_SQUARE, 0.0)
    slots[OFFSETS] = jnp.full((2, LANES), FAR, F32)
    for half in range(2):
        halo[half, OFFSETS * 64 :, :] = jnp.zeros((64, LANES), BF16)
    acc[...] = jnp.zeros((3, 64, LANES), F32)
    low = lax.broadcasted_iota(jnp.int32, (1, LANES), 1) < 64
    hot_row = lax.broadcasted_iota(jnp.int32, (32, LANES), 0).astype(F32)
    for copy in loads:
        copy.wait()
    embed_wide = embed[...].astype(F32)
    tables = []
    for g in range(2):
        rows = [radial_one[g, n : n + 1, :] * embed_wide for n in range(4)]
        tables.append(jnp.concatenate(rows, axis=0).astype(BF16))
    table_scalar, table_vector = tables

    expected = OFFSETS - 1
    if COMPACT:
        expected = expected + OFFSETS
        for flag in selves.values():
            expected = expected - jnp.where(flag, 1, 0)
    pl.semaphore_wait(barrier, expected)
    for o in farthest + [CENTRE]:
        elsewhere(o, lambda o=o: coordinates(o).start())

    def keep_packet(o):
        slots[o] = packet[...]

    for o in range(OFFSETS):
        at_home(o, functools.partial(keep_packet, o))
    for o in range(OFFSETS):
        elsewhere(o, lambda o=o: coordinates(o).wait_recv())

    own_packet = slots[CENTRE]
    column = jnp.transpose(jnp.concatenate([own_packet, jnp.zeros((6, LANES), F32)], axis=0))
    own_cols = [column[0:64, 0:1], column[64:LANES, 0:1], column[0:64, 1:2]]
    own_kind = column[64:LANES, 1:2]
    live_col = jnp.where(own_kind >= 0.0, 1.0, 0.0)
    for k in range(3):
        place = jnp.where(live_col > 0.0, own_cols[k], -FAR)
        own[k] = jnp.broadcast_to(place, (64, LANES))
    live_row = jnp.where(own_packet[1:2, 64:LANES] >= 0.0, 1.0, 0.0)
    species_id = lax.broadcasted_iota(jnp.int32, (64, 8), 1).astype(F32)
    own_hot = jnp.where(own_kind == species_id, 1.0, 0.0).astype(BF16)
    own_embed = nn(own_hot, embed[...])

    def parts(o):
        return o // 9 - 1, lax.rem(o // 3, 3) - 1, lax.rem(o, 3) - 1

    def far_rows(m):
        first, second = slots[2 * m], slots[2 * m + 1]
        first_turned, second_turned = pltpu.roll(first, 64, 1), pltpu.roll(second, 64, 1)
        shift_first, shift_second = parts(2 * m), parts(2 * m + 1)
        pairs = (
            (first[0:1], second_turned[0:1]),
            (first_turned[0:1], second[0:1]),
            (first[1:2], second_turned[1:2]),
        )
        rows = []
        for k, (a, b) in enumerate(pairs):
            a = a + shift_first[k].astype(F32) * CELL_SIDE
            b = b + shift_second[k].astype(F32) * CELL_SIDE
            rows.append(jnp.where(low, a, b))
        return rows, jnp.where(low, first_turned[1:2], second[1:2])

    def geometry(places, m, top):
        rows = pl.ds(top, PIECE)
        sep = [places[k] - own[k, rows, :] for k in range(3)]
        dist = sep[0] * sep[0] + sep[1] * sep[1] + sep[2] * sep[2] + SOFTEN
        self_pair = jnp.where(m == CENTRE // 2, 1.0, 0.0)
        dist = jnp.minimum(dist + diag[rows, :] * self_pair, CUT_SQUARE)
        inverse = lax.rsqrt(dist)
        edge = (CUT_SQUARE - dist) * (1.0 / CUT_SQUARE)
        angle = dist * inverse * WAVE - 0.5 * math.pi
        sine, minus_cosine = cos_sin(angle)
        double = -2.0 * minus_cosine
        sines = [sine, double * sine]
        sines.append(double * sines[1] - sines[0])
        sines.append(double * sines[2] - sines[1])
        return sep, inverse, edge, sines, double

    def forward(m, carry):
        places, kinds = far_rows(m)
        for n in range(4):
            hit = jnp.where(kinds == hot_row - 8.0 * n, 1.0, 0.0).astype(BF16)
            hot[:, pl.ds(pl.multiple_of(m * 512 + n * LANES, LANES), LANES)] = hit
        for top in range(0, 64, PIECE):
            sep, inverse, edge, sines, _ = geometry(places, m, top)
            weight = edge * edge * inverse
            scaled = inverse * ROOT_THREE
            units = [s * scaled for s in sep]
            for n in range(4):
                basis = sines[n] * weight
                narrow = basis.astype(BF16)
                wide_cols = pl.ds(pl.multiple_of(m * 512 + n * LANES, LANES), LANES)
                cols = pl.ds(pl.multiple_of(m * LANES, LANES), LANES)
                sm[n * 64 + top : n * 64 + top + PIECE, cols] = narrow
                vs[top : top + PIECE, wide_cols] = narrow
                for k in range(3):
                    at = 64 * (k + 1) + top
                    vs[at : at + PIECE, wide_cols] = (units[k] * basis).astype(BF16)
        return carry

    def gather_kinds(m):
        cols = pl.ds(pl.multiple_of(m * 512, 512), 512)
        tally[...] += nt(vs[:, cols], hot[:, cols])

    def forward_next(m, carry):
        gather_kinds(m - 1)
        return forward(m, carry)

    tally[...] = jnp.zeros((256, 32), F32)
    forward(jnp.int32(0), 0)
    lax.fori_loop(1, CHUNKS, forward_next, 0)
    gather_kinds(jnp.int32(CHUNKS - 1))
    kinds_sum = tally[...]
    high = kinds_sum.astype(BF16)
    rest = (kinds_sum - high.astype(F32)).astype(BF16)
    scalar_msg = MSG_SCALE * (nn(high[0:64], table_scalar) + nn(rest[0:64], table_scalar))
    vector_msg = MSG_SCALE * (nn(high[64:], table_vector) + nn(rest[64:], table_vector))
    squares = vector_msg * vector_msg
    norm = squares[0:64] + squares[64:128] + squares[128:192]
    invariants = jnp.concatenate([scalar_msg, norm], axis=1).astype(BF16)
    mixing = nt(invariants, mix_one[...])
    gate = sigmoid(mixing)
    layer_one = (own_embed + mixing * gate).astype(BF16)
    mine[0] = layer_one
    halo[0, CENTRE * 64 : CENTRE * 64 + 64, :] = layer_one
    for o in farthest:
        channels(1, o).start()

    def slopes(m, carry):
        places, _ = far_rows(m)
        cols = pl.ds(pl.multiple_of(m * LANES, LANES), LANES)
        for top in range(0, 64, PIECE):
            sep, inverse, edge, sines, double = geometry(places, m, top)
            weight = edge * edge * inverse
            fall = -edge * (4.0 / CUT_SQUARE + edge * inverse * inverse)
            cosines = [0.5 * double, 0.5 * double * double - 1.0]
            cosines.append(double * cosines[1] - cosines[0])
            cosines.append(double * cosines[2] - cosines[1])
            rows = pl.ds(top, PIECE)
            for k in range(3):
                pre[k, rows, cols] = sep[k]
            pre[3, rows, cols] = inverse
            for n in range(4):
                pre[4 + n, rows, cols] = sines[n] * weight
                turn = cosines[n] * ((n + 1) * WAVE)
                pre[8 + n, rows, cols] = turn * weight + sines[n] * fall
        return carry

    lax.fori_loop(0, CHUNKS, slopes, 0)
    for o in neighbours:
        channels(1, o).wait_recv()

    def spread(half):
        def step(j, total):
            rows = pl.ds(pl.multiple_of(j * 256, 256), 256)
            return total + nn(sm[:, rows], halo[half, rows, :])

        total = lax.fori_loop(0, 7, step, jnp.zeros((256, LANES), F32))
        result = None
        for n in range(4):
            term = total[n * 64 : n * 64 + 64] * (MSG_SCALE * radial_two[n : n + 1, :])
            result = term if result is None else result + term
        return result

    rounded_two = spread(0).astype(BF16)
    mixing_two = nt(rounded_two, mix_two[...])
    gate_two = sigmoid(mixing_two)
    layer_wide = layer_one.astype(F32)
    features = (layer_wide + mixing_two * gate_two).astype(BF16)
    hidden = nt(features, read_hidden[...])
    slope = silu_slope(hidden, sigmoid(hidden)) * read_out[...] * live_col
    feature_adjoint = nn(slope.astype(BF16), read_hidden[...])
    mixing_adjoint = (feature_adjoint * silu_slope(mixing_two, gate_two)).astype(BF16)
    rounded_adjoint = nn(mixing_adjoint, mix_two[...]).astype(BF16)
    mine[1] = rounded_adjoint
    halo[1, CENTRE * 64 : CENTRE * 64 + 64, :] = rounded_adjoint
    for o in farthest:
        channels(2, o).start()

    sheet_out[...] = features

    def keep_sheet():
        sheet_in[...] = sheet_out[...]

    second = hidden * sigmoid(hidden) * read_out[...]
    second = jnp.concatenate([second, jnp.zeros((64, LANES - 16), F32)], axis=1)
    energy = jnp.transpose(layer_wide * read_one[...] + second)
    energy = jnp.sum(energy, axis=0, keepdims=True) * live_row
    adjoint_wide = rounded_adjoint.astype(F32)
    for n in range(4):
        scale = MSG_SCALE * radial_two[n : n + 1, :]
        pair_lhs[n * 64 : n * 64 + 64, 0:LANES] = (scale * adjoint_wide).astype(BF16)
        pair_lhs[n * 64 : n * 64 + 64, LANES:] = (scale * layer_wide).astype(BF16)
    for o in neighbours:
        channels(2, o).wait_recv()
    elsewhere(CENTRE, lambda: sheet().start())
    at_home(CENTRE, keep_sheet)

    layer_adjoint = feature_adjoint + read_one[...] * live_col + spread(1)
    mixing_one_adjoint = (layer_adjoint * silu_slope(mixing, gate)).astype(BF16)
    invariant_adjoint = nn(mixing_one_adjoint, mix_one[...])
    scalar_adjoint = (MSG_SCALE * invariant_adjoint[:, 0:LANES]).astype(BF16)
    norm_adjoint = (2.0 * MSG_SCALE) * invariant_adjoint[:, LANES:]
    vector_adjoint = jnp.concatenate(
        [vector_msg[k * 64 : k * 64 + 64] * norm_adjoint for k in range(3)], axis=0
    ).astype(BF16)
    kinds_adjoint = jnp.concatenate(
        [nt(scalar_adjoint, table_scalar), nt(vector_adjoint, table_vector)], axis=0
    ).astype(BF16)

    def pulls_of(m, way):
        wide_cols = pl.ds(pl.multiple_of(m * 512, 512), 512)
        d1[way] = nn(kinds_adjoint, hot[:, wide_cols])

    def backward_one(m, way):
        cols = pl.ds(pl.multiple_of(m * LANES, LANES), LANES)
        ghost = [jnp.zeros((PIECE, LANES), F32) for _ in range(3)]
        for top in range(0, 64, PIECE):
            rows = pl.ds(top, PIECE)
            sep = [pre[k, rows, cols] for k in range(3)]
            inverse = pre[3, rows, cols]
            scaled = inverse * ROOT_THREE
            along, across = None, None
            turned = [None, None, None]
            for n in range(4):
                basis, slope_n = pre[4 + n, rows, cols], pre[8 + n, rows, cols]
                lanes = slice(n * LANES, (n + 1) * LANES)
                pulls = [
                    d1[way, 64 * (k + 1) + top : 64 * (k + 1) + top + PIECE, lanes]
                    for k in range(3)
                ]
                projected = sep[0] * pulls[0] + sep[1] * pulls[1] + sep[2] * pulls[2]
                push = (d1[way, top : top + PIECE, lanes] + scaled * projected) * slope_n
                along = push if along is None else along + push
                lean = basis * projected
                across = lean if across is None else across + lean
                for k in range(3):
                    term = basis * pulls[k]
                    turned[k] = term if turned[k] is None else turned[k] + term
            radial = inverse * (along - scaled * inverse * across)
            for k in range(3):
                grad = sep[k] * radial + scaled * turned[k]
                ghost[k] = ghost[k] + grad
                acc[k, rows, :] = acc[k, rows, :] - grad
        row = [jnp.sum(ghost[k], axis=0, keepdims=True) for k in range(3)]
        turned = [pltpu.roll(row[k], 64, 1) for k in range(3)]
        ghosts_out[2 * m, 0:1, :] = jnp.where(low, row[0], turned[1])
        ghosts_out[2 * m, 1:2, :] = jnp.where(low, row[2], 0.0)
        ghosts_out[2 * m + 1, 0:1, :] = jnp.where(low, turned[0], row[1])
        ghosts_out[2 * m + 1, 1:2, :] = jnp.where(low, turned[2], 0.0)

    pulls_of(jnp.int32(0), 0)

    def backward_pair(j, carry):
        pulls_of(2 * j + 1, 1)
        backward_one(2 * j, 0)
        pulls_of(jnp.minimum(2 * j + 2, CHUNKS - 1), 0)
        backward_one(2 * j + 1, 1)
        return carry

    lax.fori_loop(0, CHUNKS // 2, backward_pair, 0)

    def keep_ghosts(o):
        ghosts_in[o] = ghosts_out[o]

    for o in farthest:
        elsewhere(o, lambda o=o: ghosts(o).start())
    for o in neighbours:
        at_home(o, functools.partial(keep_ghosts, o))

    def backward_two(m, carry):
        cols = pl.ds(pl.multiple_of(m * LANES, LANES), LANES)
        far_channels = jnp.concatenate([halo[0, cols, :], halo[1, cols, :]], axis=1)
        d1[0, :, 0:LANES] = nt(pair_lhs[...], far_channels)
        for top in range(0, 64, PIECE):
            rows = pl.ds(top, PIECE)
            along = None
            for n in range(4):
                push = d1[0, n * 64 + top : n * 64 + top + PIECE, 0:LANES] * pre[8 + n, rows, cols]
                along = push if along is None else along + push
            along = along * pre[3, rows, cols]
            for k in range(3):
                acc[k, rows, :] = acc[k, rows, :] - along * pre[k, rows, cols]
        return carry

    lax.fori_loop(0, CHUNKS, backward_two, 0)
    sums = [jnp.sum(jnp.transpose(acc[k]), axis=0, keepdims=True) for k in range(3)]
    centre_out[0:1, :] = ghosts_out[CENTRE, 0:1, :] + jnp.concatenate(sums[0:2], axis=1)
    centre_out[1:2, :] = ghosts_out[CENTRE, 1:2, :] + jnp.concatenate([sums[2], energy], axis=1)

    def keep_centre():
        ghosts_in[CENTRE] = centre_out[...]

    elsewhere(CENTRE, lambda: ghosts(CENTRE).start())
    at_home(CENTRE, keep_centre)
    elsewhere(CENTRE, lambda: sheet().wait_recv())
    features_out[0, 0, 0] = sheet_in[...]
    for o in neighbours:
        elsewhere(o, lambda o=o: ghosts(o).wait_recv())
    total = ghosts_in[0]
    for o in neighbours[1:]:
        total = total + ghosts_in[o]
    elsewhere(CENTRE, lambda: ghosts(CENTRE).wait_recv())
    centre = ghosts_in[CENTRE]
    total = -(total + centre)
    forces[0, 0, 0] = total[0:1, 0:64]
    forces[0, 0, 1] = total[0:1, 64:LANES]
    forces[0, 0, 2] = total[1:2, 0:64]
    energies[0, 0] = centre[1:2, 64:LANES]

    for o in range(OFFSETS):
        elsewhere(o, lambda o=o: coordinates(o).wait_send())
    for o in neighbours:
        channels(1, o).wait_send()
        channels(2, o).wait_send()
    elsewhere(CENTRE, lambda: sheet().wait_send())
    for o in range(OFFSETS):
        elsewhere(o, lambda o=o: ghosts(o).wait_send())


def local(
    shape,
    positions,
    species,
    counts,
    embed,
    radial_one,
    mix_one,
    read_one,
    radial_two,
    mix_two,
    read_hidden,
    read_out,
):
    weights = (
        embed,
        radial_one,
        mix_one,
        read_one[None, :],
        radial_two,
        mix_two,
        read_hidden,
        read_out[None, :],
    )
    slots = positions.shape[-1]
    vmem = pl.BlockSpec(memory_space=pltpu.VMEM)
    positions = jnp.transpose(positions, (0, 1, 3, 2, 4))
    forces, energies, features = pl.pallas_call(
        functools.partial(kernel, shape),
        out_shape=(
            jax.ShapeDtypeStruct(positions.shape, F32),
            jax.ShapeDtypeStruct(species.shape, F32),
            jax.ShapeDtypeStruct((1, 1, 1, slots, LANES), BF16),
        ),
        in_specs=[vmem, vmem, pl.BlockSpec(memory_space=pltpu.SMEM)]
        + [pl.BlockSpec(memory_space=pl.ANY)] * 8,
        out_specs=(vmem, vmem, vmem),
        scratch_shapes=[pltpu.VMEM(w.shape, w.dtype) for w in weights]
        + [
            pltpu.VMEM((2, LANES), F32),
            pltpu.VMEM((OFFSETS + 1, 2, LANES), F32),
            pltpu.VMEM((2, CHUNKS * LANES, LANES), BF16),
            pltpu.VMEM((2, 64, LANES), BF16),
            pltpu.VMEM((64, LANES), BF16),
            pltpu.VMEM((64, LANES), BF16),
            pltpu.VMEM((OFFSETS + 1, 2, LANES), F32),
            pltpu.VMEM((2, LANES), F32),
            pltpu.VMEM((OFFSETS, 2, LANES), F32),
            pltpu.VMEM((3, 64, LANES), F32),
            pltpu.VMEM((64, LANES), F32),
            pltpu.VMEM((256, CHUNKS * 512), BF16),
            pltpu.VMEM((256, CHUNKS * LANES), BF16),
            pltpu.VMEM((32, CHUNKS * 512), BF16),
            pltpu.VMEM((12, 64, CHUNKS * LANES), F32),
            pltpu.VMEM((2, 256, 512), F32),
            pltpu.VMEM((3, 64, LANES), F32),
            pltpu.VMEM((256, 2 * LANES), BF16),
            pltpu.VMEM((256, 32), F32),
            pltpu.SemaphoreType.DMA((4, OFFSETS)),
            pltpu.SemaphoreType.DMA((4, OFFSETS)),
            pltpu.SemaphoreType.DMA((8,)),
        ],
        compiler_params=pltpu.CompilerParams(
            collective_id=0, has_side_effects=True, vmem_limit_bytes=60 * 1024 * 1024
        ),
        name="potential",
    )(positions, species, counts, *weights)
    forces = jnp.transpose(forces, (0, 1, 3, 2, 4))
    return forces, energies, jnp.swapaxes(features, 3, 4)


def solution(mesh):
    shape = tuple(mesh.shape[name] for name in ("gx", "gy", "gz"))
    block = ("gx", "gy", "gz")
    in_specs = (P(*block, None, None), P(*block, None), P(*block)) + (P(),) * 8
    out_specs = (P(*block, None, None), P(*block, None), P(*block, None, None))
    step = functools.partial(local, shape)
    return jax.shard_map(step, mesh=mesh, in_specs=in_specs, out_specs=out_specs, check_vma=False)
```

time: 102 us -> 66.6 us (0.65)
  starting transfers between devices: 32.4 us -> 0 us
  Pallas kernels: 50.7 us -> 61.9 us
  waiting for transfers between devices: 9.18 us -> 0 us
  local copies, waits for them, and re-layouts: 6.03 us -> 3.07 us
  other arithmetic: 1.43 us -> 0 us
    ppermute x3 -> x0, starting transfers between devices: 32.4 us -> none  [moved(): lax.ppermute(value, ('gx', 'gz'), permutation(shape))]
    pallas_call x1, Pallas kernels: 50.7 us -> 61.9 us  [local(): pl.pallas_call(functools.partial(kernel, shape), out_shape=(jax.ShapeDtyp...]
    ppermute x3 -> x0, waiting for transfers between devices: 9.18 us -> none  [moved(): lax.ppermute(value, ('gx', 'gz'), permutation(shape))]
    unnamed x18 -> x7, local copies, waits for them, and re-layouts: 4.78 us -> 3.07 us
  transfers between devices with their start and end apart: 3 -> 0, of which waited for: 2 -> 0; matrix products, arithmetic and copies ran while one was open for 2% -> 0% of each run, Pallas kernels for 0% -> 0%
where the time goes in v1:
time: 66.6 us; the launch traced here: 66.3 us
  Pallas kernels  61.9 us (93%)
  local copies, waits for them, and re-layouts  3.07 us (5%)
  between operations  1.3 us (2%)
    pallas_call x1, Pallas kernels, local(): pl.pallas_call(functools.partial(kernel, shape), out_shape=(jax.ShapeDtyp...  61.9 us
    unnamed x7, local copies, waits for them, and re-layouts  3.07 us

profile of v1, /device:TPU:16, one launch (start us, length us, event | category | flops | bytes accessed | tf_op | source)
XLA Modules:
  0.0 66.3 jit_solution(9109263406354082816)
XLA Ops:
  1.3 61.9 %potential.1 = (f32[1,1,3,1,64]{4,3,2,1,0:T(1,128)}, f32[1,1,1,64]{3,2,1,0:T(1,128)}, bf16[1,1,1,64,128]{4,3,2,1,0:T(8,128)(2,1)}) custom-call(f32[1,1,3,1,64]{4,3,2,1,0:T(1,128)} %bitcast.8, s32[1,1,1,64]{3,2,1,0:T(1,128)} %species.1, s32[1,1,1]{2,1,0:T(1,128)S(6)} %copy.18.counts, bf16[8,128]{1,0:T(8,128)(2,1)} %refs_0_.1, f32[2,4,128]{2,1,0:T(4,128)} %refs_1_.1, ...), custom_call_target="tpu_custom_call" | custom-call | tf_op jit(solution)/shard_map/potential/pallas_call | solution.py:572
  63.2 0.0 copy-start
  63.2 0.6 copy-done
  63.9 0.0 copy-start.1
  63.9 0.6 copy.19
  64.4 0.0 copy-done.1
  64.5 0.5 copy.20
  65.0 1.3 %copy.21 = bf16[1,1,1,128,64]{3,4,2,1,0:T(8,128)(2,1)} copy(bf16[1,1,1,128,64]{3,4,2,1,0:T(8,128)(2,1)} %bitcast.7) | data formatting | bytes 32768
Async XLA Ops:
  63.2 0.6 copy-start
  63.9 0.6 copy-start.1

commit v2 on v1

--- a/solution.py
+++ b/solution.py
@@ -17,6 +17,7 @@
 FAR = 1000.0
 MESH = pl.DeviceIdType.MESH
 OFFSETS = 27
+OPERANDS = 11
 CENTRE = 13
 CHUNKS = 14
 LANES = 128
@@ -57,16 +58,29 @@
     return o // 9 - 1, o // 3 % 3 - 1, o % 3 - 1
 
 
+def meets_itself(shape, o):
+    nx, ny, nz = shape
+    run = nx // nz
+    ox, oy, oz = corner(o)
+    for gx in range(nx):
+        for gz in range(nz):
+            bx, bz = gz * run + gx % run, (gx // run + nz // 2) % nz
+            if (bx + ox - gx) % nx == 0 and oy % ny == 0 and (bz + oz - gz) % nz == 0:
+                return True
+    return False
+
+
 def kernel(
     shape,
-    positions,
-    species,
-    counts,
     *refs,
 ):
-    sources, refs = refs[:8], refs[8:]
+    sources, refs = refs[:OPERANDS], refs[OPERANDS:]
     forces, energies, features_out = refs[:3]
+    staged = refs[3 : 3 + OPERANDS]
     (
+        positions,
+        species,
+        counts,
         embed,
         radial_one,
         mix_one,
@@ -75,7 +89,7 @@
         mix_two,
         read_hidden,
         read_out,
-    ) = refs[3:11]
+    ) = staged
     (
         packet,
         slots,
@@ -99,7 +113,7 @@
         send,
         recv,
         load,
-    ) = refs[11:]
+    ) = refs[3 + OPERANDS :]
     nx, ny, nz = shape
     here = (lax.axis_index("gx"), lax.axis_index("gy"), lax.axis_index("gz"))
 
@@ -113,7 +127,12 @@
         )
 
     if COMPACT:
-        block = (here[2] * run + lax.rem(here[0], run), here[1], here[0] // run)
+        turned = here[0] // run + nz // 2
+        block = (
+            here[2] * run + lax.rem(here[0], run),
+            here[1],
+            jnp.where(turned >= nz, turned - nz, turned),
+        )
     else:
         block = here
     block_near = [near(index, size) for index, size in zip(block, shape)]
@@ -128,8 +147,16 @@
         if not COMPACT:
             return bx, by, bz
         low_x, high_x = halves[1 + ox]
-        return bz * run + low_x, by, high_x
-
+        return triples[2][4 + oz] * run + low_x, by, high_x
+
+    def far_side(three):
+        return three + tuple(
+            jnp.where(v + nz // 2 >= nz, v + nz // 2 - nz, v + nz // 2) for v in three
+        )
+
+    if COMPACT:
+        block_near[2] = far_side(block_near[2])
+        here_near[2] = far_side(here_near[2])
     block_halves = splits(block_near[0]) if COMPACT else None
     here_halves = splits(here_near[0]) if COMPACT else None
 
@@ -152,7 +179,7 @@
     selves = {}
     if COMPACT:
         for o in range(OFFSETS):
-            if corner(o)[1] == 0 or ny < 3:
+            if meets_itself(shape, o):
                 selves[o] = is_here(holders[o])
 
     def elsewhere(o, action):
@@ -193,6 +220,11 @@
     def sheet():
         return remote(sheet_out, sheet_in, 1, CENTRE, holders[CENTRE])
 
+    loads = []
+    for i in range(OPERANDS):
+        copy = pltpu.make_async_copy(sources[i], staged[i], load.at[i])
+        copy.start()
+        loads.append(copy)
     barrier = pltpu.get_barrier_semaphore()
 
     def greet(device):
@@ -204,12 +236,8 @@
     for o in neighbours:
         greet(to_worker[o])
 
-    loads = []
-    for i in range(8):
-        dst = refs[3 + i]
-        copy = pltpu.make_async_copy(sources[i], dst, load.at[i])
-        copy.start()
-        loads.append(copy)
+    for copy in loads[:3]:
+        copy.wait()
     occupied = lax.broadcasted_iota(jnp.int32, (1, 64), 1) < counts[0, 0, 0]
     kinds = jnp.where(occupied, species[0, 0], -1).astype(F32)
     places = [jnp.where(occupied, positions[0, 0, k], FAR) for k in range(3)]
@@ -226,7 +254,7 @@
     acc[...] = jnp.zeros((3, 64, LANES), F32)
     low = lax.broadcasted_iota(jnp.int32, (1, LANES), 1) < 64
     hot_row = lax.broadcasted_iota(jnp.int32, (32, LANES), 0).astype(F32)
-    for copy in loads:
+    for copy in loads[3:]:
         copy.wait()
     embed_wide = embed[...].astype(F32)
     tables = []
@@ -542,6 +570,11 @@
         elsewhere(o, lambda o=o: ghosts(o).wait_send())
 
 
+def hand_over(*refs):
+    for source, target in zip(refs[:3], refs[3:]):
+        target[...] = source[...]
+
+
 def local(
     shape,
     positions,
@@ -556,7 +589,10 @@
     read_hidden,
     read_out,
 ):
-    weights = (
+    operands = (
+        jnp.transpose(positions, (0, 1, 3, 2, 4)),
+        species,
+        counts,
         embed,
         radial_one,
         mix_one,
@@ -568,18 +604,18 @@
     )
     slots = positions.shape[-1]
     vmem = pl.BlockSpec(memory_space=pltpu.VMEM)
-    positions = jnp.transpose(positions, (0, 1, 3, 2, 4))
     forces, energies, features = pl.pallas_call(
         functools.partial(kernel, shape),
         out_shape=(
-            jax.ShapeDtypeStruct(positions.shape, F32),
+            jax.ShapeDtypeStruct(operands[0].shape, F32),
             jax.ShapeDtypeStruct(species.shape, F32),
             jax.ShapeDtypeStruct((1, 1, 1, slots, LANES), BF16),
         ),
-        in_specs=[vmem, vmem, pl.BlockSpec(memory_space=pltpu.SMEM)]
-        + [pl.BlockSpec(memory_space=pl.ANY)] * 8,
+        in_specs=[pl.BlockSpec(memory_space=pltpu.HBM)] * OPERANDS,
         out_specs=(vmem, vmem, vmem),
-        scratch_shapes=[pltpu.VMEM(w.shape, w.dtype) for w in weights]
+        scratch_shapes=[
+            (pltpu.SMEM if w is counts else pltpu.VMEM)(w.shape, w.dtype) for w in operands
+        ]
         + [
             pltpu.VMEM((2, LANES), F32),
             pltpu.VMEM((OFFSETS + 1, 2, LANES), F32),
@@ -602,13 +638,22 @@
             pltpu.VMEM((256, 32), F32),
             pltpu.SemaphoreType.DMA((4, OFFSETS)),
             pltpu.SemaphoreType.DMA((4, OFFSETS)),
-            pltpu.SemaphoreType.DMA((8,)),
+            pltpu.SemaphoreType.DMA((OPERANDS,)),
         ],
         compiler_params=pltpu.CompilerParams(
             collective_id=0, has_side_effects=True, vmem_limit_bytes=60 * 1024 * 1024
         ),
         name="potential",
-    )(positions, species, counts, *weights)
+    )(*operands)
+    results = (forces, energies, features)
+    forces, energies, features = pl.pallas_call(
+        hand_over,
+        out_shape=tuple(jax.ShapeDtypeStruct(r.shape, r.dtype) for r in results),
+        in_specs=[vmem] * 3,
+        out_specs=(vmem, vmem, vmem),
+        compiler_params=pltpu.CompilerParams(vmem_limit_bytes=60 * 1024 * 1024),
+        name="hand_over",
+    )(*results)
     forces = jnp.transpose(forces, (0, 1, 3, 2, 4))
     return forces, energies, jnp.swapaxes(features, 3, 4)
 

time: 66.6 us -> 61.6 us (0.925)
  local copies, waits for them, and re-layouts: 3.07 us -> 0 us
  Pallas kernels: 61.9 us -> 60.1 us
    pallas_call x1, Pallas kernels: 61.9 us -> 58.8 us  [local(): pl.pallas_call(functools.partial(kernel, shape), out_shape=(jax.ShapeDtyp...]
    unnamed x7 -> x0, local copies, waits for them, and re-layouts: 3.07 us -> none
    pallas_call x0 -> x1, Pallas kernels: none -> 1.34 us  [local(): pl.pallas_call(hand_over, out_shape=tuple((jax.ShapeDtypeStruct(r.shape,...]
where the time goes in v2:
time: 61.6 us; the launch traced here: 61.4 us
  Pallas kernels  60.1 us (98%)
  between operations  1.29 us (2%)
    pallas_call x1, Pallas kernels, local(): pl.pallas_call(functools.partial(kernel, shape), out_shape=(jax.ShapeDtyp...  58.8 us
    pallas_call x1, Pallas kernels, local(): pl.pallas_call(hand_over, out_shape=tuple((jax.ShapeDtypeStruct(r.shape,...  1.34 us

profile of v2, /device:TPU:16, one launch (start us, length us, event | category | flops | bytes accessed | tf_op | source)
XLA Modules:
  0.0 61.4 jit_solution(12975621031525979478)
XLA Ops:
  1.3 58.8 %potential.1 = (f32[1,1,3,1,64]{4,3,2,1,0:T(1,128)}, f32[1,1,1,64]{3,2,1,0:T(1,128)}, bf16[1,1,1,64,128]{4,3,2,1,0:T(8,128)(2,1)}) custom-call(f32[1,1,3,1,64]{4,3,2,1,0:T(1,128)} %bitcast.7, s32[1,1,1,64]{3,2,1,0:T(1,128)} %refs_1_.1, s32[1,1,1]{2,1,0:T(1,128)S(6)} %copy.15.refs_2_, bf16[8,128]{1,0:T(8,128)(2,1)} %refs_3_.1, f32[2,4,128]{2,1,0:T(4,128)} %refs_4_.1, ...), custom_call_target="tpu_custom_call" | custom-call | tf_op jit(solution)/shard_map/potential/pallas_call | solution.py:607
  60.1 1.3 %hand_over.1 = (f32[1,1,3,1,64]{4,3,2,1,0:T(1,128)}, f32[1,1,1,64]{3,2,1,0:T(1,128)}, bf16[1,1,1,64,128]{4,3,2,1,0:T(8,128)(2,1)}) custom-call(f32[1,1,3,1,64]{4,3,2,1,0:T(1,128)} %get-tuple-element.9.refs_0_, f32[1,1,1,64]{3,2,1,0:T(1,128)} %get-tuple-element.10.refs_1_, bf16[1,1,1,64,128]{4,3,2,1,0:T(8,128)(2,1)} %get-tuple-element.11.refs_2_), custom_call_target="tpu_custom_call" | custom-call | tf_op jit(solution)/shard_map/hand_over/pallas_call | solution.py:649

commit v3 on v2

--- a/solution.py
+++ b/solution.py
@@ -18,7 +18,8 @@
 MESH = pl.DeviceIdType.MESH
 OFFSETS = 27
 OPERANDS = 11
-CENTRE = 13
+CENTRE = 4
+EARLY = 4
 CHUNKS = 14
 LANES = 128
 PIECE = 16
@@ -55,7 +56,7 @@
 
 
 def corner(o):
-    return o // 9 - 1, o // 3 % 3 - 1, o % 3 - 1
+    return o // 3 % 3 - 1, o % 3 - 1, (0, -1, 1)[o // 9]
 
 
 def meets_itself(shape, o):
@@ -165,7 +166,7 @@
         return block_near[0][1 + ox], block_near[1][1 + oy], block_near[2][1 + oz]
 
     def opposite(o):
-        return OFFSETS - 1 - o
+        return (0, 2, 1)[o // 9] * 9 + 8 - o % 9
 
     def is_here(device):
         same = (device[0] == here[0]) & (device[1] == here[1])
@@ -247,7 +248,7 @@
     packet[1:2, 64:LANES] = kinds
     row_id = lax.broadcasted_iota(jnp.int32, (64, LANES), 0)
     lane_id = lax.broadcasted_iota(jnp.int32, (64, LANES), 1)
-    diag[...] = jnp.where(row_id + 64 == lane_id, CUT_SQUARE, 0.0)
+    diag[...] = jnp.where(row_id == lane_id, CUT_SQUARE, 0.0)
     slots[OFFSETS] = jnp.full((2, LANES), FAR, F32)
     for half in range(2):
         halo[half, OFFSETS * 64 :, :] = jnp.zeros((64, LANES), BF16)
@@ -277,7 +278,7 @@
 
     for o in range(OFFSETS):
         at_home(o, functools.partial(keep_packet, o))
-    for o in range(OFFSETS):
+    for o in range(9):
         elsewhere(o, lambda o=o: coordinates(o).wait_recv())
 
     own_packet = slots[CENTRE]
@@ -294,7 +295,9 @@
     own_embed = nn(own_hot, embed[...])
 
     def parts(o):
-        return o // 9 - 1, lax.rem(o // 3, 3) - 1, lax.rem(o, 3) - 1
+        layer = o // 9
+        step = jnp.where(layer == 0, 0, jnp.where(layer == 1, -1, 1))
+        return lax.rem(o // 3, 3) - 1, lax.rem(o, 3) - 1, step
 
     def far_rows(m):
         first, second = slots[2 * m], slots[2 * m + 1]
@@ -352,17 +355,20 @@
 
     def gather_kinds(m):
         cols = pl.ds(pl.multiple_of(m * 512, 512), 512)
-        tally[...] += nt(vs[:, cols], hot[:, cols])
+        tally[...] += nt(hot[:, cols], vs[:, cols])
 
     def forward_next(m, carry):
         gather_kinds(m - 1)
         return forward(m, carry)
 
-    tally[...] = jnp.zeros((256, 32), F32)
+    tally[...] = jnp.zeros((32, 256), F32)
     forward(jnp.int32(0), 0)
-    lax.fori_loop(1, CHUNKS, forward_next, 0)
+    lax.fori_loop(1, EARLY, forward_next, 0)
+    for o in range(9, OFFSETS):
+        elsewhere(o, lambda o=o: coordinates(o).wait_recv())
+    lax.fori_loop(EARLY, CHUNKS, forward_next, 0)
     gather_kinds(jnp.int32(CHUNKS - 1))
-    kinds_sum = tally[...]
+    kinds_sum = jnp.transpose(tally[...])
     high = kinds_sum.astype(BF16)
     rest = (kinds_sum - high.astype(F32)).astype(BF16)
     scalar_msg = MSG_SCALE * (nn(high[0:64], table_scalar) + nn(rest[0:64], table_scalar))
@@ -390,7 +396,7 @@
             cosines.append(double * cosines[2] - cosines[1])
             rows = pl.ds(top, PIECE)
             for k in range(3):
-                pre[k, rows, cols] = sep[k]
+                pre[k, rows, cols] = sep[k] * (inverse * ROOT_THREE)
             pre[3, rows, cols] = inverse
             for n in range(4):
                 pre[4 + n, rows, cols] = sines[n] * weight
@@ -469,7 +475,7 @@
         ghost = [jnp.zeros((PIECE, LANES), F32) for _ in range(3)]
         for top in range(0, 64, PIECE):
             rows = pl.ds(top, PIECE)
-            sep = [pre[k, rows, cols] for k in range(3)]
+            unit = [pre[k, rows, cols] for k in range(3)]
             inverse = pre[3, rows, cols]
             scaled = inverse * ROOT_THREE
             along, across = None, None
@@ -481,17 +487,17 @@
                     d1[way, 64 * (k + 1) + top : 64 * (k + 1) + top + PIECE, lanes]
                     for k in range(3)
                 ]
-                projected = sep[0] * pulls[0] + sep[1] * pulls[1] + sep[2] * pulls[2]
-                push = (d1[way, top : top + PIECE, lanes] + scaled * projected) * slope_n
+                projected = unit[0] * pulls[0] + unit[1] * pulls[1] + unit[2] * pulls[2]
+                push = (d1[way, top : top + PIECE, lanes] + projected) * slope_n
                 along = push if along is None else along + push
                 lean = basis * projected
                 across = lean if across is None else across + lean
                 for k in range(3):
                     term = basis * pulls[k]
                     turned[k] = term if turned[k] is None else turned[k] + term
-            radial = inverse * (along - scaled * inverse * across)
+            radial = (along - inverse * across) * (1.0 / ROOT_THREE)
             for k in range(3):
-                grad = sep[k] * radial + scaled * turned[k]
+                grad = unit[k] * radial + scaled * turned[k]
                 ghost[k] = ghost[k] + grad
                 acc[k, rows, :] = acc[k, rows, :] - grad
         row = [jnp.sum(ghost[k], axis=0, keepdims=True) for k in range(3)]
@@ -510,15 +516,23 @@
         backward_one(2 * j + 1, 1)
         return carry
 
-    lax.fori_loop(0, CHUNKS // 2, backward_pair, 0)
 
     def keep_ghosts(o):
         ghosts_in[o] = ghosts_out[o]
 
-    for o in farthest:
-        elsewhere(o, lambda o=o: ghosts(o).start())
-    for o in neighbours:
-        at_home(o, functools.partial(keep_ghosts, o))
+    def send_ghosts(first, last):
+        for o in farthest:
+            if first <= o < last:
+                elsewhere(o, lambda o=o: ghosts(o).start())
+        for o in neighbours:
+            if first <= o < last:
+                at_home(o, functools.partial(keep_ghosts, o))
+
+    split = 4
+    lax.fori_loop(0, split, backward_pair, 0)
+    send_ghosts(0, 4 * split)
+    lax.fori_loop(split, CHUNKS // 2, backward_pair, 0)
+    send_ghosts(4 * split, OFFSETS)
 
     def backward_two(m, carry):
         cols = pl.ds(pl.multiple_of(m * LANES, LANES), LANES)
@@ -530,7 +544,7 @@
             for n in range(4):
                 push = d1[0, n * 64 + top : n * 64 + top + PIECE, 0:LANES] * pre[8 + n, rows, cols]
                 along = push if along is None else along + push
-            along = along * pre[3, rows, cols]
+            along = along * (1.0 / ROOT_THREE)
             for k in range(3):
                 acc[k, rows, :] = acc[k, rows, :] - along * pre[k, rows, cols]
         return carry
@@ -635,7 +649,7 @@
             pltpu.VMEM((2, 256, 512), F32),
             pltpu.VMEM((3, 64, LANES), F32),
             pltpu.VMEM((256, 2 * LANES), BF16),
-            pltpu.VMEM((256, 32), F32),
+            pltpu.VMEM((32, 256), F32),
             pltpu.SemaphoreType.DMA((4, OFFSETS)),
             pltpu.SemaphoreType.DMA((4, OFFSETS)),
             pltpu.SemaphoreType.DMA((OPERANDS,)),

time: 61.6 us -> 60.9 us (0.989)
  Pallas kernels: 60.1 us -> 59.4 us
    pallas_call x1, Pallas kernels: 58.8 us -> 58.1 us  [local(): pl.pallas_call(functools.partial(kernel, shape), out_shape=(jax.ShapeDtyp...]
where the time goes in v3:
time: 60.9 us; the launch traced here: 60.7 us
  Pallas kernels  59.4 us (98%)
  between operations  1.29 us (2%)
    pallas_call x1, Pallas kernels, local(): pl.pallas_call(functools.partial(kernel, shape), out_shape=(jax.ShapeDtyp...  58.1 us
    pallas_call x1, Pallas kernels, local(): pl.pallas_call(hand_over, out_shape=tuple((jax.ShapeDtypeStruct(r.shape,...  1.34 us

profile of v3, /device:TPU:16, one launch (start us, length us, event | category | flops | bytes accessed | tf_op | source)
XLA Modules:
  0.0 60.7 jit_solution(3095824760254516475)
XLA Ops:
  1.3 58.1 %potential.1 = (f32[1,1,3,1,64]{4,3,2,1,0:T(1,128)}, f32[1,1,1,64]{3,2,1,0:T(1,128)}, bf16[1,1,1,64,128]{4,3,2,1,0:T(8,128)(2,1)}) custom-call(f32[1,1,3,1,64]{4,3,2,1,0:T(1,128)} %bitcast.7, s32[1,1,1,64]{3,2,1,0:T(1,128)} %refs_1_.1, s32[1,1,1]{2,1,0:T(1,128)S(6)} %copy.15.refs_2_, bf16[8,128]{1,0:T(8,128)(2,1)} %refs_3_.1, f32[2,4,128]{2,1,0:T(4,128)} %refs_4_.1, ...), custom_call_target="tpu_custom_call" | custom-call | tf_op jit(solution)/shard_map/potential/pallas_call | solution.py:621
  59.4 1.3 %hand_over.1 = (f32[1,1,3,1,64]{4,3,2,1,0:T(1,128)}, f32[1,1,1,64]{3,2,1,0:T(1,128)}, bf16[1,1,1,64,128]{4,3,2,1,0:T(8,128)(2,1)}) custom-call(f32[1,1,3,1,64]{4,3,2,1,0:T(1,128)} %get-tuple-element.9.refs_0_, f32[1,1,1,64]{3,2,1,0:T(1,128)} %get-tuple-element.10.refs_1_, bf16[1,1,1,64,128]{4,3,2,1,0:T(8,128)(2,1)} %get-tuple-element.11.refs_2_), custom_call_target="tpu_custom_call" | custom-call | tf_op jit(solution)/shard_map/hand_over/pallas_call | solution.py:663

commit v4 on v3

--- a/solution.py
+++ b/solution.py
@@ -270,7 +270,7 @@
         for flag in selves.values():
             expected = expected - jnp.where(flag, 1, 0)
     pl.semaphore_wait(barrier, expected)
-    for o in farthest + [CENTRE]:
+    for o in range(OFFSETS):
         elsewhere(o, lambda o=o: coordinates(o).start())
 
     def keep_packet(o):
@@ -405,15 +405,20 @@
         return carry
 
     lax.fori_loop(0, CHUNKS, slopes, 0)
-    for o in neighbours:
-        channels(1, o).wait_recv()
 
     def spread(half):
         def step(j, total):
             rows = pl.ds(pl.multiple_of(j * 256, 256), 256)
             return total + nn(sm[:, rows], halo[half, rows, :])
 
-        total = lax.fori_loop(0, 7, step, jnp.zeros((256, LANES), F32))
+        for o in neighbours:
+            if o < 9:
+                channels(1 + half, o).wait_recv()
+        total = lax.fori_loop(0, 2, step, jnp.zeros((256, LANES), F32))
+        for o in neighbours:
+            if o >= 9:
+                channels(1 + half, o).wait_recv()
+        total = lax.fori_loop(2, 7, step, total)
         result = None
         for n in range(4):
             term = total[n * 64 : n * 64 + 64] * (MSG_SCALE * radial_two[n : n + 1, :])
@@ -449,12 +454,11 @@
         scale = MSG_SCALE * radial_two[n : n + 1, :]
         pair_lhs[n * 64 : n * 64 + 64, 0:LANES] = (scale * adjoint_wide).astype(BF16)
         pair_lhs[n * 64 : n * 64 + 64, LANES:] = (scale * layer_wide).astype(BF16)
-    for o in neighbours:
-        channels(2, o).wait_recv()
+    total_adjoint = spread(1)
     elsewhere(CENTRE, lambda: sheet().start())
     at_home(CENTRE, keep_sheet)
 
-    layer_adjoint = feature_adjoint + read_one[...] * live_col + spread(1)
+    layer_adjoint = feature_adjoint + read_one[...] * live_col + total_adjoint
     mixing_one_adjoint = (layer_adjoint * silu_slope(mixing, gate)).astype(BF16)
     invariant_adjoint = nn(mixing_one_adjoint, mix_one[...])
     scalar_adjoint = (MSG_SCALE * invariant_adjoint[:, 0:LANES]).astype(BF16)

time: 60.9 us -> 60.8 us (level)
  no operation moved by 1% of the time
where the time goes in v4:
time: 60.8 us; the launch traced here: 60.6 us
  Pallas kernels  59.3 us (98%)
  between operations  1.29 us (2%)
    pallas_call x1, Pallas kernels, local(): pl.pallas_call(functools.partial(kernel, shape), out_shape=(jax.ShapeDtyp...  57.9 us
    pallas_call x1, Pallas kernels, local(): pl.pallas_call(hand_over, out_shape=tuple((jax.ShapeDtypeStruct(r.shape,...  1.34 us

profile of v4, /device:TPU:16, one launch (start us, length us, event | category | flops | bytes accessed | tf_op | source)
XLA Modules:
  0.0 60.6 jit_solution(7418597702715936718)
XLA Ops:
  1.3 57.9 %potential.1 = (f32[1,1,3,1,64]{4,3,2,1,0:T(1,128)}, f32[1,1,1,64]{3,2,1,0:T(1,128)}, bf16[1,1,1,64,128]{4,3,2,1,0:T(8,128)(2,1)}) custom-call(f32[1,1,3,1,64]{4,3,2,1,0:T(1,128)} %bitcast.7, s32[1,1,1,64]{3,2,1,0:T(1,128)} %refs_1_.1, s32[1,1,1]{2,1,0:T(1,128)S(6)} %copy.15.refs_2_, bf16[8,128]{1,0:T(8,128)(2,1)} %refs_3_.1, f32[2,4,128]{2,1,0:T(4,128)} %refs_4_.1, ...), custom_call_target="tpu_custom_call" | custom-call | tf_op jit(solution)/shard_map/potential/pallas_call | solution.py:625
  59.2 1.3 %hand_over.1 = (f32[1,1,3,1,64]{4,3,2,1,0:T(1,128)}, f32[1,1,1,64]{3,2,1,0:T(1,128)}, bf16[1,1,1,64,128]{4,3,2,1,0:T(8,128)(2,1)}) custom-call(f32[1,1,3,1,64]{4,3,2,1,0:T(1,128)} %get-tuple-element.9.refs_0_, f32[1,1,1,64]{3,2,1,0:T(1,128)} %get-tuple-element.10.refs_1_, bf16[1,1,1,64,128]{4,3,2,1,0:T(8,128)(2,1)} %get-tuple-element.11.refs_2_), custom_call_target="tpu_custom_call" | custom-call | tf_op jit(solution)/shard_map/hand_over/pallas_call | solution.py:667
